TPU v7x, 128 devices: a whole 4x4x4 slice. The times are simulated.
128 devices in a mesh: tm: 32 (over x, z, core), panel: 4 (over y).
Axes of the slice: x: 4, y: 4, z: 4, core: 2. Of those that a mesh axis runs over, the one named last changes fastest.
Arguments:
- design: bfloat16 [8192, 7680], P('tm', 'panel'), may hold values from -6 to 6
- partials: bfloat16 [8192, 64], P('tm'), may hold values from -0.119628906 to 0.119628906
- observed: bfloat16 [8192], P('tm'), may hold values from -6 to 6
- arc_of_row: int32 [8192, 1], replicated, may hold values from 0 to 31, as said below
- autoreg: float32 [32], replicated, may hold values from -0.55 to 0.5
- movavg: float32 [32], replicated, may hold values from 0.3 to 0.9
Outputs:
- normal: float32 [7680, 7680], P('tm', 'panel')
- right_hand: float32 [7680], P('panel')
Inputs may be any that keep to these rules, and one draw needn't show every extreme that they name: arc_of_row never falls along the epochs and names every arc; arcs 2b and 2b + 1 together have 2 * 256 epochs, one of them 384 // 3 to 160 epochs and the other 352 to 384; one arc has exactly 384 epochs and its partner exactly 128, so that at most 12 rows of one device belong to one arc, and every device holds exactly 12 rows of the longest arc; arc a is held by index a of tm.
All inputs are finite; a program needn't handle non-finite values.
Results may differ from a plain program's by a relative error of at most 0.02.
Values may be sent and summed in bfloat16 or wider, within the bound.
A program may use at most 192 MiB of HBM per device.

v0:
```python
import jax
import jax.numpy as jnp
from jax import lax
from jax.sharding import PartitionSpec as P


def whiten_matrix(order_row, order_col, usable_row, usable_col, ar_value, ma_value):
    spacing = order_row[:, None] - order_col[None, :]
    lag_steps = jnp.maximum(spacing - 1, 0)
    parity = (lag_steps % 2).astype(jnp.float32)
    flip_sign = 1.0 - 2.0 * parity
    decayed = (
        -(ar_value + ma_value)
        * flip_sign
        * jnp.exp(lag_steps.astype(jnp.float32) * jnp.log(ma_value))
    )
    entry = jnp.where(spacing == 0, jnp.float32(1.0), decayed)
    allowed = usable_row[:, None] & usable_col[None, :] & (spacing >= 0)
    return jnp.where(allowed, entry, jnp.float32(0.0)).astype(jnp.bfloat16)


def eliminate(whitener, rows_design, rows_params, rows_obs, scale):
    white_design = jnp.dot(whitener, rows_design, preferred_element_type=jnp.float32)
    white_params = jnp.dot(whitener, rows_params, preferred_element_type=jnp.float32)
    white_obs = jnp.dot(whitener, rows_obs, preferred_element_type=jnp.float32)
    param_count = rows_params.shape[1]
    param_gram = jnp.dot(white_params.T, white_params, precision=lax.Precision.HIGHEST) + jnp.eye(
        param_count, dtype=jnp.float32
    )
    factor = jnp.linalg.cholesky(param_gram)
    basis = lax.linalg.triangular_solve(factor, white_params.T, left_side=True, lower=True)
    arc_terms = jnp.dot(basis, white_design, precision=lax.Precision.HIGHEST)
    arc_rhs = jnp.dot(basis, white_obs, precision=lax.Precision.HIGHEST)
    right_part = (
        jnp.dot(white_design.T, white_obs, precision=lax.Precision.HIGHEST)
        - jnp.dot(arc_terms.T, arc_rhs, precision=lax.Precision.HIGHEST)
    ) * scale
    return (white_design.astype(jnp.bfloat16), arc_terms.astype(jnp.bfloat16), right_part)


def body(design, partials, observed, arc_of_row, autoreg, movavg):
    tile_count = lax.axis_size("tm")
    device_index = lax.axis_index("tm")
    rows_dev = design.shape[0]
    panel_width = design.shape[1]
    param_count = partials.shape[1]
    capacity = 3 * rows_dev // 2 // tile_count
    slot_count = tile_count * capacity
    scale = 1.0 / (rows_dev * tile_count)
    arc_ids = arc_of_row[:, 0]
    epoch_table = arc_ids.reshape(rows_dev, tile_count)
    local_arcs = lax.dynamic_slice_in_dim(epoch_table, device_index, 1, 1)[:, 0]
    onehot = (local_arcs[:, None] == jnp.arange(tile_count, dtype=jnp.int32)[None, :]).astype(
        jnp.int32
    )
    earlier = jnp.cumsum(onehot, axis=0) - onehot
    within = jnp.sum(earlier * onehot, axis=1)
    target_slot = local_arcs * capacity + within
    source_row = (
        jnp.zeros((slot_count,), jnp.int32)
        .at[target_slot]
        .set(jnp.arange(1, rows_dev + 1, dtype=jnp.int32))
    )

    def pick_rows(values):
        padded = jnp.concatenate([jnp.zeros((1,) + values.shape[1:], values.dtype), values], axis=0)
        return jnp.take(padded, source_row, axis=0)

    send_design = pick_rows(design).reshape(tile_count, capacity, panel_width)
    send_params = pick_rows(partials).reshape(tile_count, capacity, param_count)
    send_obs = pick_rows(observed).reshape(tile_count, capacity)
    got_design, got_params, got_obs = (
        lax.all_to_all(send_design, "tm", split_axis=0, concat_axis=0, tiled=True),
        lax.all_to_all(send_params, "tm", split_axis=0, concat_axis=0, tiled=True),
        lax.all_to_all(send_obs, "tm", split_axis=0, concat_axis=0, tiled=True),
    )
    got_design = got_design.reshape(slot_count, panel_width)
    got_params = got_params.reshape(slot_count, param_count)
    got_obs = got_obs.reshape(slot_count)
    per_source = jnp.sum((epoch_table == device_index).astype(jnp.int32), axis=0)
    arc_start = jnp.sum((arc_ids < device_index).astype(jnp.int32))
    first_pos = jnp.mod(jnp.arange(tile_count, dtype=jnp.int32) - arc_start, tile_count)
    offset_in = jnp.arange(capacity, dtype=jnp.int32)
    order_pos = (first_pos[:, None] + offset_in[None, :] * tile_count).reshape(slot_count)
    usable = (offset_in[None, :] < per_source[:, None]).reshape(slot_count)
    whitener = whiten_matrix(
        order_pos, order_pos, usable, usable, autoreg[device_index], movavg[device_index]
    )
    design_bf, terms_bf, right_part = eliminate(whitener, got_design, got_params, got_obs, scale)
    right_hand = lax.psum(right_part, "tm")
    own_rows = jnp.concatenate([design_bf, terms_bf], axis=0)
    signed_rows = jnp.concatenate([design_bf, -terms_bf], axis=0)
    gathered = lax.all_gather(signed_rows, "panel", axis=1, tiled=True)
    product = lax.dot_general(
        gathered, own_rows, (((0,), (0,)), ((), ())), preferred_element_type=jnp.float32
    )
    normal = lax.psum_scatter(
        (product * scale).astype(jnp.bfloat16), "tm", scatter_dimension=0, tiled=True
    ).astype(jnp.float32)
    return (normal, right_hand)


def solution(mesh):
    in_specs = (P("tm", "panel"), P("tm", None), P("tm"), P(), P(), P())
    out_specs = (P("tm", "panel"), P("panel"))
    return jax.shard_map(body, mesh=mesh, in_specs=in_specs, out_specs=out_specs, check_vma=False)
```

profile of v0, /device:TPU:1, one launch (start us, length us, event | category | flops | bytes accessed | tf_op | source)
XLA Modules:
  0.0 332.8 jit_solution(6460968665628124426)
XLA Ops:
  7.2 1.0 copy.16
  8.1 0.5 broadcast.193
  8.7 2.1 fusion.33
  10.8 0.1 reshape_squeeze.3
  10.9 0.0 copy-start.1
  10.9 0.2 dynamic-slice_reduce_fusion
  11.1 0.6 reduce-window.6
  11.7 0.2 slice_reduce_fusion
  11.9 0.1 fusion.36
  12.0 0.1 copy.15
  12.2 0.2 fusion.31
  12.4 1.4 scatter_custom_fusion
  13.8 0.7 pad_maximum_fusion.1
  14.5 2.8 gather_fusion.2
  17.4 0.1 broadcast_in_dim.54
  17.5 1.4 gather_fusion.1
  19.0 0.1 broadcast_select_fusion.1
  19.2 0.8 reshape.233
  19.9 9.4 %all-to-all-start.1 = ((bf16[32,2,384]{2,1,0:T(2,128)(2,1)}), bf16[32,2,384]{2,1,0:T(2,128)(2,1)S(1)}, u32[]{:S(2)}, u32[]{:S(2)}) async-start(bf16[32,2,384]{2,1,0:T(2,128)(2,1)} %reshape.233), calls=%async_computation.1 | async-start | bytes 98304 | tf_op jit(solution)/shard_map/all_to_all | solution.py:74
  29.4 0.7 and_select_fusion
  30.0 0.2 concatenate.15
  30.3 2.5 gather_fusion
  32.8 0.4 gather.17
  33.2 1.6 broadcast_select_fusion
  34.7 0.1 broadcast_add_fusion
  34.8 0.1 convert_reduce_fusion
  34.9 1.8 all-to-all-done.1
  36.7 5.6 %all-to-all-start = ((bf16[32,12,1920]{2,1,0:T(8,128)(2,1)}), bf16[32,12,1920]{2,1,0:T(8,128)(2,1)S(1)}, u32[]{:S(2)}, u32[]{:S(2)}) async-start(bf16[32,12,1920]{2,1,0:T(8,128)(2,1)} %broadcast_select_fusion), calls=%async_computation | async-start | bytes 3932160 | tf_op jit(solution)/shard_map/all_to_all | solution.py:73
  42.3 0.2 all-gather.2.cloned.1.call-start
  42.5 0.1 iota_compare_fusion.5
  42.6 0.6 dynamic_slice.10
  43.9 0.6 dynamic_slice.9
  45.8 0.1 add.112
  45.9 0.1 lt.72
  46.0 0.1 reshape.234
  46.2 0.7 fusion.27
  46.9 0.2 fusion.69
  47.2 0.1 copy.17
  47.3 5.8 %cholesky.17 = f32[64,64]{1,0:T(8,128)S(1)} custom-call(f32[64,64]{1,0:T(8,128)S(1)} %fusion.40), custom_call_target="Cholesky" | custom-call | tf_op jit(solution)/shard_map/jit(cholesky)/cholesky | solution.py:30
  53.2 0.6 compare_reduce_fusion
  53.8 0.7 fusion.32
  54.5 4.9 %custom-call.6 = f32[1,64,64]{1,2,0:T(8,128)S(1)} custom-call(f32[1,64,64]{2,1,0:T(8,128)S(1)} %fusion.32), custom_call_target="InvertDiagBlocksLowerTriangular" | custom-call | tf_op jit(solution)/shard_map/triangular_solve | solution.py:31
  59.4 0.3 fusion.37
  59.7 9.5 %all-to-all-done = bf16[32,12,1920]{2,1,0:T(8,128)(2,1)S(1)} async-done(((bf16[32,12,1920]{2,1,0:T(8,128)(2,1)}), bf16[32,12,1920]{2,1,0:T(8,128)(2,1)S(1)}, u32[]{:S(2)}, u32[]{:S(2)}) %all-to-all-start) | async-done | bytes 1474592 | tf_op jit(solution)/shard_map/all_to_all | solution.py:73
  69.2 1.3 reshape.165
  70.5 2.7 fusion.68
  73.2 2.3 fusion.67
  75.6 1.3 pad_maximum_fusion
  76.9 0.0 all-gather.2.cloned.1.call-update
  76.9 0.0 reduce-scatter.4.cloned.1.call-start
  76.9 68.3 %all-gather.2.cloned.1.call-done = bf16[448,7680]{1,0:T(8,128)(2,1)} async-done(((bf16[448,1920]{1,0:T(8,128)(2,1)}), bf16[448,7680]{1,0:T(8,128)(2,1)}) %all-gather.2.cloned.1.call-update) | async-done | bytes 6881296 | tf_op jit(solution)/shard_map/all_gather | solution.py:93
  145.3 22.9 %multiply_convert_fusion = bf16[7680,1920]{1,0:T(8,128)(2,1)} fusion(bf16[448,7680]{1,0:T(8,128)(2,1)} %all-gather.2.cloned.1.call-done, bf16[64,1920]{1,0:T(8,128)(2,1)} %get-tuple-element.7, bf16[384,1920]{1,0:T(8,128)(2,1)} %copy-done), kind=kOutput, calls=%fused_computation.4 | convolution fusion | flops 13244989440 | bytes 38092800 | tf_op jit(solution)/shard_map/dot_general | solution.py:94
  168.1 0.0 reduce-scatter.4.cloned.1.call-update
  168.2 0.7 select_n.84
  168.9 14.5 %all_to_all.16 = bf16[32,1,12]{2,1,0:T(2,128)(2,1)S(1)} all-to-all(bf16[32,1,12]{2,1,0:T(2,128)(2,1)} %select_n.84), channel_id=1, replica_groups=mesh['tm'=32,'panel'=4] {'tm'}, dimensions={0} | all-to-all | bytes 1536 | tf_op jit(solution)/shard_map/all_to_all | solution.py:75
  183.4 0.7 reduce.12
  184.1 0.8 reshape.203
  184.9 1.5 convolution_bitcast_fusion
  186.3 0.2 convolution_bitcast_fusion.1
  186.5 0.4 convolution_reduce_fusion
  187.0 1.7 fusion.5
  188.7 65.3 %psum.7 = f32[1920]{0:T(1024)} all-reduce(f32[1920]{0:T(1024)S(1)} %subtract_multiply_fusion), channel_id=1, replica_groups=mesh['tm'=32,'panel'=4] {'tm'}, use_global_device_ids=true, to_apply=%region_9.10 | all-reduce | flops 1920 | bytes 15360 | tf_op jit(solution)/shard_map/psum | solution.py:90
  254.0 69.5 %reduce-scatter.4.cloned.1.call-done = bf16[240,1920]{1,0:T(8,128)(2,1)} async-done(((bf16[7680,1920]{1,0:T(8,128)(2,1)}), bf16[240,1920]{1,0:T(8,128)(2,1)}) %reduce-scatter.4.cloned.1.call-update) | async-done | bytes 921616
  323.4 2.5 convert_element_type.57
  (29 shorter events, 0.3 us)
Async XLA Ops:
  7.2 22.9 %copy-start.3 = (bf16[256,1920]{1,0:T(8,128)(2,1)S(1)}, bf16[256,1920]{1,0:T(8,128)(2,1)}, u32[]{:S(2)}) copy-start(bf16[256,1920]{1,0:T(8,128)(2,1)} %param.6) | copy-start | bytes 2949124
  10.9 2.9 copy-start.1
  19.9 16.7 %all-to-all-start.1 = ((bf16[32,2,384]{2,1,0:T(2,128)(2,1)}), bf16[32,2,384]{2,1,0:T(2,128)(2,1)S(1)}, u32[]{:S(2)}, u32[]{:S(2)}) async-start(bf16[32,2,384]{2,1,0:T(2,128)(2,1)} %reshape.233), calls=%async_computation.1 | async-start | bytes 98304 | tf_op jit(solution)/shard_map/all_to_all | solution.py:74
  33.2 1.7 copy-start.2
  34.9 7.7 %copy-start.6 = (f32[32]{0:T(128)S(1)}, f32[32]{0:T(128)}, u32[]{:S(2)}) copy-start(f32[32]{0:T(128)} %param.11) | copy-start | bytes 388
  34.9 9.0 %copy-start.7 = (f32[32]{0:T(128)S(1)}, f32[32]{0:T(128)}, u32[]{:S(2)}) copy-start(f32[32]{0:T(128)} %param.10) | copy-start | bytes 388
  36.7 32.5 %all-to-all-start = ((bf16[32,12,1920]{2,1,0:T(8,128)(2,1)}), bf16[32,12,1920]{2,1,0:T(8,128)(2,1)S(1)}, u32[]{:S(2)}, u32[]{:S(2)}) async-start(bf16[32,12,1920]{2,1,0:T(8,128)(2,1)} %broadcast_select_fusion), calls=%async_computation | async-start | bytes 3932160 | tf_op jit(solution)/shard_map/all_to_all | solution.py:73
  42.3 103.0 %all-gather.2.cloned.1.call-start = ((), (), s32[]{:S(2)}) async-start(), calls=%async_computation.4 | async-start | bytes 8601600 | tf_op jit(solution)/shard_map/all_gather | solution.py:93
  45.9 24.6 %copy-start.4 = (s32[384]{0:T(512)}, s32[384]{0:T(512)S(1)}, u32[]{:S(2)}) copy-start(s32[384]{0:T(512)S(1)} %add.112) | copy-start | bytes 4612
  46.0 24.5 %copy-start.5 = (pred[384]{0:T(512)(128)(4,1)}, pred[384]{0:T(512)(128)(4,1)S(1)}, u32[]{:S(2)}) copy-start(pred[384]{0:T(512)(128)(4,1)S(1)} %lt.72) | copy-start | bytes 1156
  73.2 2.4 copy-start
  76.9 246.6 %reduce-scatter.4.cloned.1.call-start = ((), (), s32[]{:S(2)}) async-start(), calls=%async_computation.5 | async-start | bytes 30412800
Sparse Core Ops, SparseCore 0:
  77.0 68.1 all-gather.1
  168.3 155.1 reduce-scatter.3
where the time goes:
time: 333 us
  waiting for transfers between devices  149 us (45%)
  blocking collectives  79.9 us (24%)
  matrix products  33 us (10%)
  other arithmetic  23 us (7%)
  between operations  16.4 us (5%)
  local copies, waits for them, and re-layouts  16.2 us (5%)
  starting transfers between devices  15.3 us (5%)
    unnamed x3, waiting for transfers between devices  69.5 us
    all_gather x1, waiting for transfers between devices, body(): gathered = lax.all_gather(signed_rows, 'panel', axis=1, tiled=True)  68.3 us
    psum x1, blocking collectives, body(): right_hand = lax.psum(right_part, 'tm')  65.3 us
    dot_general x1, matrix products, body(): lax.dot_general(gathered, own_rows, (((0,), (0,)), ((), ())), preferred_e...  22.9 us
    all_to_all x1, blocking collectives, body(): lax.all_to_all(send_obs, 'tm', split_axis=0, concat_axis=0, tiled=True)  14.5 us
    all_to_all x1, waiting for transfers between devices, body(): lax.all_to_all(send_design, 'tm', split_axis=0, concat_axis=0, tiled=True)  9.49 us
    all_to_all x1, starting transfers between devices, body(): lax.all_to_all(send_params, 'tm', split_axis=0, concat_axis=0, tiled=True)  9.43 us
    gather x5, local copies, waits for them, and re-layouts, pick_rows(): return jnp.take(padded, source_row, axis=0)  7.16 us
  transfers between devices with their start and end apart: 4, of which 4 were waited for; matrix products, arithmetic and copies ran while one was open for 8% of the time, Pallas kernels for 0%

commit v1 on v0

--- a/solution.py
+++ b/solution.py
@@ -2,6 +2,11 @@
 import jax.numpy as jnp
 from jax import lax
 from jax.sharding import PartitionSpec as P
+
+
+def gather_from_all(x, axis, dim):
+    copies = jnp.concatenate([x] * lax.axis_size(axis), axis=dim)
+    return lax.all_to_all(copies, axis, dim, dim, tiled=True)
 
 
 def whiten_matrix(order_row, order_col, usable_row, usable_col, ar_value, ma_value):
@@ -90,7 +95,7 @@
     right_hand = lax.psum(right_part, "tm")
     own_rows = jnp.concatenate([design_bf, terms_bf], axis=0)
     signed_rows = jnp.concatenate([design_bf, -terms_bf], axis=0)
-    gathered = lax.all_gather(signed_rows, "panel", axis=1, tiled=True)
+    gathered = gather_from_all(signed_rows, "panel", 1)
     product = lax.dot_general(
         gathered, own_rows, (((0,), (0,)), ((), ())), preferred_element_type=jnp.float32
     )

time: 333 us -> 396 us (1.19)
  blocking collectives: 79.9 us -> 158 us
  waiting for transfers between devices: 149 us -> 77.3 us
  other arithmetic: 23 us -> 71.9 us
  local copies, waits for them, and re-layouts: 16.2 us -> 20.4 us
    all_to_all x0 -> x1, blocking collectives: none -> 80.2 us  [gather_from_all(): return lax.all_to_all(copies, axis, dim, dim, tiled=True)]
    all_gather x1 -> x0, waiting for transfers between devices: 68.3 us -> none  [body(): gathered = lax.all_gather(signed_rows, 'panel', axis=1, tiled=True)]
    concatenate x1, other arithmetic: 1.31 us -> 49.4 us  [gather_from_all(): copies = jnp.concatenate([x] * lax.axis_size(axis), axis=dim)]
    unnamed x3 -> x2, waiting for transfers between devices: 69.5 us -> 67.7 us
  transfers between devices with their start and end apart: 4 -> 3, of which waited for: 4 -> 2; matrix products, arithmetic and copies ran while one was open for 8% -> 7% of each run, Pallas kernels for 0% -> 0%
where the time goes in v1:
time: 396 us; the launch traced here: 395 us
  blocking collectives  158 us (40%)
  waiting for transfers between devices  77.3 us (20%)
  other arithmetic  71.9 us (18%)
  matrix products  34 us (9%)
  local copies, waits for them, and re-layouts  20.4 us (5%)
  starting transfers between devices  16.9 us (4%)
  between operations  16.4 us (4%)
    all_to_all x1, blocking collectives, gather_from_all(): return lax.all_to_all(copies, axis, dim, dim, tiled=True)  80.2 us
    unnamed x2, waiting for transfers between devices  67.7 us
    psum x1, blocking collectives, body(): right_hand = lax.psum(right_part, 'tm')  65.3 us
    concatenate x1, other arithmetic, gather_from_all(): copies = jnp.concatenate([x] * lax.axis_size(axis), axis=dim)  49.4 us
    dot_general x1, matrix products, body(): lax.dot_general(gathered, own_rows, (((0,), (0,)), ((), ())), preferred_e...  26 us
    all_to_all x1, blocking collectives, body(): lax.all_to_all(send_obs, 'tm', split_axis=0, concat_axis=0, tiled=True)  12.9 us
    all_to_all x1, waiting for transfers between devices, body(): lax.all_to_all(send_design, 'tm', split_axis=0, concat_axis=0, tiled=True)  9.66 us
    all_to_all x1, starting transfers between devices, body(): lax.all_to_all(send_params, 'tm', split_axis=0, concat_axis=0, tiled=True)  9.43 us
  transfers between devices with their start and end apart: 3, of which 2 were waited for; matrix products, arithmetic and copies ran while one was open for 7% of the time, Pallas kernels for 0%

profile of v1, /device:TPU:1, one launch (start us, length us, event | category | flops | bytes accessed | tf_op | source)
XLA Modules:
  0.0 395.4 jit_solution(2891118962664698615)
XLA Ops:
  7.2 0.9 copy.22
  8.1 0.5 broadcast.193
  8.6 2.1 fusion.33
  10.7 0.1 reshape_squeeze.3
  10.8 0.0 copy-start.4
  10.8 0.2 dynamic-slice_reduce_fusion
  11.0 0.6 reduce-window.6
  11.6 0.2 slice_reduce_fusion
  11.8 0.1 fusion.36
  11.9 0.1 copy.21
  12.1 0.2 fusion.31
  12.3 1.4 scatter_custom_fusion
  13.7 0.7 pad_maximum_fusion
  14.5 2.8 gather_fusion.2
  17.3 0.1 broadcast_in_dim.54
  17.4 1.4 gather_fusion.1
  18.9 0.1 broadcast_select_fusion.1
  19.1 0.8 reshape.235
  19.8 9.4 %all-to-all-start.1 = ((bf16[32,2,384]{2,1,0:T(2,128)(2,1)}), bf16[32,2,384]{2,1,0:T(2,128)(2,1)S(1)}, u32[]{:S(2)}, u32[]{:S(2)}) async-start(bf16[32,2,384]{2,1,0:T(2,128)(2,1)} %reshape.235), calls=%async_computation.1 | async-start | bytes 98304 | tf_op jit(solution)/shard_map/all_to_all | solution.py:79
  29.3 0.7 and_select_fusion
  29.9 1.4 concatenate.18
  31.4 2.5 gather_fusion
  33.9 0.0 copy-start.8
  33.9 0.4 gather.17
  34.3 1.6 broadcast_select_fusion
  35.9 0.1 broadcast_add_fusion
  35.9 1.0 convert_reduce_fusion
  36.9 7.4 %all-to-all-start = ((bf16[32,12,1920]{2,1,0:T(8,128)(2,1)}), bf16[32,12,1920]{2,1,0:T(8,128)(2,1)S(1)}, u32[]{:S(2)}, u32[]{:S(2)}) async-start(bf16[32,12,1920]{2,1,0:T(8,128)(2,1)} %broadcast_select_fusion), calls=%async_computation | async-start | bytes 3932160 | tf_op jit(solution)/shard_map/all_to_all | solution.py:78
  44.3 0.0 reduce-scatter.4.cloned.1.call-start
  44.3 0.1 iota_compare_fusion.5
  44.4 0.6 dynamic_slice.10
  45.7 0.6 dynamic_slice.9
  47.6 0.1 add.112
  47.7 0.1 lt.72
  47.8 0.1 reshape.236
  48.0 0.7 fusion.27
  48.8 0.2 fusion.69
  49.0 0.1 copy.23
  49.1 5.8 %cholesky.17 = f32[64,64]{1,0:T(8,128)S(1)} custom-call(f32[64,64]{1,0:T(8,128)S(1)} %fusion.40), custom_call_target="Cholesky" | custom-call | tf_op jit(solution)/shard_map/jit(cholesky)/cholesky | solution.py:35
  55.0 0.6 compare_reduce_fusion
  55.6 0.7 fusion.32
  56.3 4.9 %custom-call.6 = f32[1,64,64]{1,2,0:T(8,128)S(1)} custom-call(f32[1,64,64]{2,1,0:T(8,128)S(1)} %fusion.32), custom_call_target="InvertDiagBlocksLowerTriangular" | custom-call | tf_op jit(solution)/shard_map/triangular_solve | solution.py:36
  61.2 0.3 fusion.37
  61.5 9.7 %all-to-all-done = bf16[32,12,1920]{2,1,0:T(8,128)(2,1)S(1)} async-done(((bf16[32,12,1920]{2,1,0:T(8,128)(2,1)}), bf16[32,12,1920]{2,1,0:T(8,128)(2,1)S(1)}, u32[]{:S(2)}, u32[]{:S(2)}) %all-to-all-start) | async-done | bytes 1474592 | tf_op jit(solution)/shard_map/all_to_all | solution.py:78
  71.2 0.4 reshape.167
  71.5 1.4 fusion.68
  73.0 1.7 fusion.67
  74.6 49.4 %maximum_maximum_fusion = bf16[448,7680]{1,0:T(8,128)(2,1)S(1)} fusion(bf16[64,1920]{1,0:T(8,128)(2,1)S(1)} %get-tuple-element.6, bf16[384,1920]{1,0:T(8,128)(2,1)S(1)} %get-tuple-element.9), kind=kLoop, calls=%fused_computation.6 | loop fusion | flops 55050240 | bytes 8601600 | tf_op jit(solution)/shard_map/concatenate | solution.py:8
  124.0 0.5 copy.32
  124.5 80.2 %all_to_all.28 = bf16[448,4,1920]{2,0,1:T(8,128)(2,1)S(1)} all-to-all(bf16[448,4,1920]{2,0,1:T(8,128)(2,1)S(1)} %bitcast.70), channel_id=1, replica_groups=mesh['tm'=32,'panel'=4] {'panel'}, dimensions={1} | all-to-all | bytes 13762560 | tf_op jit(solution)/shard_map/all_to_all | solution.py:9
  204.8 3.4 copy.29
  208.2 26.0 %multiply_convert_fusion = bf16[7680,1920]{1,0:T(8,128)(2,1)} fusion(bf16[448,7680]{1,0:T(8,128)(2,1)} %bitcast.72, bf16[64,1920]{1,0:T(8,128)(2,1)S(1)} %get-tuple-element.7, bf16[384,1920]{1,0:T(8,128)(2,1)S(1)} %copy-done.3), kind=kOutput, calls=%fused_computation.4 | convolution fusion | flops 13244989440 | bytes 38092800 | tf_op jit(solution)/shard_map/dot_general | solution.py:99
  234.2 0.0 reduce-scatter.4.cloned.1.call-update
  234.2 0.7 select_n.84
  235.0 12.9 %all_to_all.29 = bf16[32,1,12]{2,1,0:T(2,128)(2,1)S(1)} all-to-all(bf16[32,1,12]{2,1,0:T(2,128)(2,1)} %select_n.84), channel_id=1, replica_groups=mesh['tm'=32,'panel'=4] {'tm'}, dimensions={0} | all-to-all | bytes 1536 | tf_op jit(solution)/shard_map/all_to_all | solution.py:80
  247.8 0.7 reduce.12
  248.5 0.8 reshape.205
  249.3 1.4 convolution_bitcast_fusion
  250.7 0.2 convolution_bitcast_fusion.1
  250.9 0.4 convolution_reduce_fusion
  251.4 1.7 fusion.5
  253.0 65.3 %psum.7 = f32[1920]{0:T(1024)} all-reduce(f32[1920]{0:T(1024)S(1)} %subtract_multiply_fusion), channel_id=1, replica_groups=mesh['tm'=32,'panel'=4] {'tm'}, use_global_device_ids=true, to_apply=%region_9.10 | all-reduce | flops 1920 | bytes 15360 | tf_op jit(solution)/shard_map/psum | solution.py:95
  318.4 67.7 %reduce-scatter.4.cloned.1.call-done = bf16[240,1920]{1,0:T(8,128)(2,1)} async-done(((bf16[7680,1920]{1,0:T(8,128)(2,1)}), bf16[240,1920]{1,0:T(8,128)(2,1)}) %reduce-scatter.4.cloned.1.call-update) | async-done | bytes 921616
  386.0 2.5 convert_element_type.57
  (31 shorter events, 0.3 us)
Async XLA Ops:
  10.8 2.9 copy-start.4
  19.8 17.1 %all-to-all-start.1 = ((bf16[32,2,384]{2,1,0:T(2,128)(2,1)}), bf16[32,2,384]{2,1,0:T(2,128)(2,1)S(1)}, u32[]{:S(2)}, u32[]{:S(2)}) async-start(bf16[32,2,384]{2,1,0:T(2,128)(2,1)} %reshape.235), calls=%async_computation.1 | async-start | bytes 98304 | tf_op jit(solution)/shard_map/all_to_all | solution.py:79
  33.9 10.5 %copy-start.7 = (f32[32]{0:T(128)S(1)}, f32[32]{0:T(128)}, u32[]{:S(2)}) copy-start(f32[32]{0:T(128)} %param.11) | copy-start | bytes 388
  33.9 11.8 %copy-start.8 = (f32[32]{0:T(128)S(1)}, f32[32]{0:T(128)}, u32[]{:S(2)}) copy-start(f32[32]{0:T(128)} %param.10) | copy-start | bytes 388
  36.9 34.3 %all-to-all-start = ((bf16[32,12,1920]{2,1,0:T(8,128)(2,1)}), bf16[32,12,1920]{2,1,0:T(8,128)(2,1)S(1)}, u32[]{:S(2)}, u32[]{:S(2)}) async-start(bf16[32,12,1920]{2,1,0:T(8,128)(2,1)} %broadcast_select_fusion), calls=%async_computation | async-start | bytes 3932160 | tf_op jit(solution)/shard_map/all_to_all | solution.py:78
  44.3 341.7 %reduce-scatter.4.cloned.1.call-start = ((), (), s32[]{:S(2)}) async-start(), calls=%async_computation.5 | async-start | bytes 30412800
  47.7 25.2 %copy-start.5 = (s32[384]{0:T(512)}, s32[384]{0:T(512)S(1)}, u32[]{:S(2)}) copy-start(s32[384]{0:T(512)S(1)} %add.112) | copy-start | bytes 4612
  47.8 25.1 %copy-start.6 = (pred[384]{0:T(512)(128)(4,1)}, pred[384]{0:T(512)(128)(4,1)S(1)}, u32[]{:S(2)}) copy-start(pred[384]{0:T(512)(128)(4,1)S(1)} %lt.72) | copy-start | bytes 1156
  72.9 1.7 copy-start
  72.9 51.0 %copy-start.2 = (bf16[384,1920]{1,0:T(8,128)(2,1)}, bf16[384,1920]{1,0:T(8,128)(2,1)S(1)}, u32[]{:S(2)}) copy-start(bf16[384,1920]{1,0:T(8,128)(2,1)S(1)} %get-tuple-element.9) | copy-start | bytes 4423684
  204.8 3.4 copy-start.3
  234.2 17.1 %copy-start.1 = (f32[384,1920]{1,0:T(8,128)S(1)}, f32[384,1920]{1,0:T(8,128)}, u32[]{:S(2)}) copy-start(f32[384,1920]{1,0:T(8,128)} %copy-done) | copy-start | bytes 8847364
Sparse Core Ops, SparseCore 0:
  234.4 151.6 reduce-scatter.3
